TPU v7x, 32 devices: a whole 2x2x4 slice. The times are simulated.
32 devices in a mesh: dp: 16 (over z, x, core), tensor: 2 (over y).
Axes of the slice: x: 2, y: 2, z: 4, core: 2. Of those that a mesh axis runs over, the one named last changes fastest.
Arguments:
- tokens: bfloat16 [320, 6144], P('dp', 'tensor'), may hold values from -6 to 6
- route_ids: int32 [320, 2], replicated, may hold values from 0 to 3, all different within a row
- route_probs: bfloat16 [320, 2], replicated, may hold values from 0.099609375 to 1
- w_gate: bfloat16 [4, 6144, 8192], P(None, 'tensor', 'dp'), may hold values from -0.078125 to 0.078125
- w_up: bfloat16 [4, 6144, 8192], P(None, 'tensor', 'dp'), may hold values from -0.078125 to 0.078125
- w_down: bfloat16 [4, 8192, 6144], P(None, 'dp', 'tensor'), may hold values from -0.0625 to 0.0625
Outputs:
- mixed_out: bfloat16 [320, 6144], P('dp', 'tensor')
Inputs may be any that keep to these rules, and one draw needn't show every extreme that they name: `route_ids`: each row names 2 different experts, and every expert is named by some row.
All inputs are finite; a program needn't handle non-finite values.
Results may differ from a plain program's by a relative error of at most 0.0049.
Values may be sent and summed in bfloat16 or wider, within the bound.
No kernel may reach another device: no remote copies, remote signals or barrier semaphores. Data moves between devices by JAX's collectives and lax.ppermute only.
A program may use at most 128 MiB of HBM per device.

v0:
```python
import jax
import jax.numpy as jnp
from jax import lax
from jax.sharding import PartitionSpec as P

BLOCK = 128


def local(tokens, route_ids, route_probs, w_gate, w_up, w_down):
    all_tokens = lax.all_gather(tokens, "dp", axis=0, tiled=True)
    token_count, top_count = route_ids.shape
    expert_count, model_width, hidden_width = w_gate.shape
    out_width = w_down.shape[2]
    pair_count = token_count * top_count
    block_count = pair_count // BLOCK + expert_count
    row_count = block_count * BLOCK
    flat_ids = route_ids.reshape(pair_count)
    expert_range = jnp.arange(expert_count, dtype=jnp.int32)
    member = (flat_ids[:, None] == expert_range[None, :]).astype(jnp.int32)
    counts = jnp.sum(member, axis=0)
    block_sizes = (counts + BLOCK - 1) // BLOCK
    block_ends = jnp.cumsum(block_sizes)
    block_starts = block_ends - block_sizes
    earlier = jnp.cumsum(member, axis=0) - member
    within = jnp.sum(earlier * member, axis=1)
    slot_index = jnp.sum(member * block_starts[None, :], axis=1) * BLOCK + within
    pair_token = jnp.arange(pair_count, dtype=jnp.int32) // top_count
    source_row = jnp.full((row_count,), token_count, jnp.int32).at[slot_index].set(pair_token)
    block_range = jnp.arange(block_count, dtype=jnp.int32)
    block_expert = jnp.sum((block_range[:, None] >= block_ends[None, :]).astype(jnp.int32), axis=1)
    block_expert = jnp.minimum(block_expert, expert_count - 1)
    pair_weight = route_probs.astype(jnp.float32).reshape(pair_count)
    slot_weight = jnp.zeros((row_count,), jnp.float32).at[slot_index].set(pair_weight)
    zero_row = jnp.zeros((1, model_width), jnp.bfloat16)
    padded_tokens = jnp.concatenate([all_tokens, zero_row], axis=0)
    token_blocks = padded_tokens[source_row].reshape(block_count, BLOCK, model_width)

    def first_pass(carry, items):
        block_tokens, expert = items
        gate_weight = lax.dynamic_index_in_dim(w_gate, expert, 0, keepdims=False)
        up_weight = lax.dynamic_index_in_dim(w_up, expert, 0, keepdims=False)
        gate_block = jnp.dot(block_tokens, gate_weight, preferred_element_type=jnp.float32)
        up_block = jnp.dot(block_tokens, up_weight, preferred_element_type=jnp.float32)
        return (carry, (gate_block, up_block))

    unused, (gate_part, up_part) = lax.scan(first_pass, 0, (token_blocks, block_expert))
    gate_part = gate_part.reshape(row_count, hidden_width)
    up_part = up_part.reshape(row_count, hidden_width)
    gate_terms, up_terms = (
        lax.all_to_all(gate_part[None], "tensor", split_axis=1, concat_axis=0, tiled=True),
        lax.all_to_all(up_part[None], "tensor", split_axis=1, concat_axis=0, tiled=True),
    )
    gate_sum = jnp.sum(gate_terms, axis=0)
    up_sum = jnp.sum(up_terms, axis=0)
    hidden_share = (gate_sum * jax.nn.sigmoid(gate_sum) * up_sum).astype(jnp.bfloat16)
    hidden = lax.all_gather(hidden_share, "tensor", axis=0, tiled=True)
    hidden_blocks = hidden.reshape(block_count, BLOCK, hidden_width)
    source_blocks = source_row.reshape(block_count, BLOCK)
    weight_blocks = slot_weight.reshape(block_count, BLOCK)

    def second_pass(mixed_acc, items):
        block_hidden, block_source, block_weight, expert = items
        down_weight = lax.dynamic_index_in_dim(w_down, expert, 0, keepdims=False)
        out_block = jnp.dot(block_hidden, down_weight, preferred_element_type=jnp.float32)
        mixed_acc = mixed_acc.at[block_source].add(out_block * block_weight[:, None])
        return (mixed_acc, 0)

    start_acc = jnp.zeros((token_count + 1, out_width), jnp.float32)
    mixed_acc, unused = lax.scan(
        second_pass, start_acc, (hidden_blocks, source_blocks, weight_blocks, block_expert)
    )
    mixed_part = mixed_acc[:token_count]
    return lax.psum_scatter(mixed_part, "dp", scatter_dimension=0, tiled=True).astype(jnp.bfloat16)


def solution(mesh):
    placed = (
        P("dp", "tensor"),
        P(),
        P(),
        P(None, "tensor", "dp"),
        P(None, "tensor", "dp"),
        P(None, "dp", "tensor"),
    )
    return jax.shard_map(
        local, mesh=mesh, in_specs=placed, out_specs=P("dp", "tensor"), check_vma=False
    )
```

profile of v0, /device:TPU:0, one launch (start us, length us, event | category | flops | bytes accessed | tf_op | source)
XLA Modules:
  0.0 436.5 jit_solution(3084232379698166312)
XLA Ops:
  10.5 4.1 scatter_custom_fusion.1
  14.7 40.0 %all-gather.6.cloned.1.call-done = bf16[16,20,3072]{2,1,0:T(8,128)(2,1)} async-done(((bf16[1,20,3072]{2,1,0:T(8,128)(2,1)}), bf16[16,20,3072]{2,1,0:T(8,128)(2,1)}) %all-gather.6.cloned.1.call-update) | async-done | bytes 1966096 | tf_op jit(solution)/shard_map/all_gather | solution.py:10
  54.7 3.9 reshape.232
  60.3 6.9 %gather_fusion = bf16[1152,3072]{1,0:T(8,128)(2,1)} fusion(bf16[321,3072]{1,0:T(8,128)(2,1)S(1)} %concatenate.3, s32[2048]{0:T(1024)S(1)} %pad_clamp_fusion), kind=kCustom, calls=%fused_computation | custom fusion | bytes 14160384 | tf_op jit(solution)/shard_map/gather | solution.py:36
  67.2 84.6 %while.22 = (s32[]{:T(128)}, f32[9,128,512]{2,1,0:T(8,128)}, f32[9,128,512]{2,1,0:T(8,128)}, bf16[9,128,3072]{2,1,0:T(8,128)(2,1)}, s32[9]{0:T(128)S(1)}, /*inde...) while((s32[]{:T(128)}, f32[9,128,512]{2,1,0:T(8,128)}, ...), condition=%wide.region_9.10_spmd, body=%wide.region_8.9_spmd.sunk | while | flops 805306368 | bytes 8390811 | solution.py:46
  69.7 3.4 fusion.61
  73.2 3.4 fusion.60
  79.1 3.5 fusion.61
  82.6 3.4 fusion.60
  88.5 3.5 fusion.61
  92.0 3.4 fusion.60
  97.9 3.4 fusion.61
  101.4 3.4 fusion.60
  107.3 3.4 fusion.61
  110.7 3.4 fusion.60
  116.7 3.5 fusion.61
  120.2 3.4 fusion.60
  126.1 3.4 fusion.61
  129.6 3.4 fusion.60
  135.5 3.4 fusion.61
  138.9 3.5 fusion.60
  144.9 3.4 fusion.61
  148.3 3.4 fusion.60
  151.8 4.8 %broadcast_in_dim_reshape.7 = f32[1,1152,512]{2,0,1:T(1,128)} reshape(f32[9,128,512]{2,1,0:T(8,128)} %get-tuple-element.80) | data formatting | bytes 4718592 | tf_op jit(solution)/shard_map/broadcast_in_dim;reshape | solution.py:50
  156.6 3.8 all-to-all-start
  160.4 4.9 %broadcast_in_dim_reshape.8 = f32[1,1152,512]{2,0,1:T(1,128)} reshape(f32[9,128,512]{2,1,0:T(8,128)} %get-tuple-element.81) | data formatting | bytes 4718592 | tf_op jit(solution)/shard_map/broadcast_in_dim;reshape | solution.py:51
  165.3 23.4 %all-to-all-done = f32[1,1152,512]{2,0,1:T(1,128)S(1)} async-done(((f32[1,1152,512]{2,0,1:T(1,128)}), f32[1,1152,512]{2,0,1:T(1,128)S(1)}, u32[]{:S(2)}, u32[]{:S(2)}) %all-to-all-start) | async-done | bytes 2359328 | tf_op jit(solution)/shard_map/all_to_all | solution.py:50
  188.7 4.9 %all-to-all-start.1 = ((f32[1,1152,512]{2,0,1:T(1,128)}), f32[1,1152,512]{2,0,1:T(1,128)}, u32[]{:S(2)}, u32[]{:S(2)}) async-start(f32[1,1152,512]{2,0,1:T(1,128)} %broadcast_in_dim_reshape.8), calls=%async_computation.1 | async-start | bytes 4718592 | tf_op jit(solution)/shard_map/all_to_all | solution.py:51
  197.4 23.8 %all-to-all-done.1 = f32[1,1152,512]{2,0,1:T(1,128)} async-done(((f32[1,1152,512]{2,0,1:T(1,128)}), f32[1,1152,512]{2,0,1:T(1,128)}, u32[]{:S(2)}, u32[]{:S(2)}) %all-to-all-start.1) | async-done | bytes 2359328 | tf_op jit(solution)/shard_map/all_to_all | solution.py:51
  227.2 4.3 scatter_custom_fusion.2
  231.5 16.1 %all-gather.4.cloned.1.call-done = bf16[1152,512]{1,0:T(8,128)(2,1)} async-done(((bf16[576,512]{1,0:T(8,128)(2,1)}), bf16[1152,512]{1,0:T(8,128)(2,1)}) %all-gather.4.cloned.1.call-update) | async-done | bytes 1179664 | tf_op jit(solution)/shard_map/all_gather | solution.py:56
  250.0 105.5 %while.23 = (s32[]{:T(128)}, f32[321,3072]{1,0:T(8,128)}, s32[9,128]{1,0:T(8,128)S(1)}, bf16[9,128,512]{2,1,0:T(8,128)(2,1)}, s32[9]{0:T(128)S(1)}, /*index=5*/b...) while((s32[]{:T(128)}, f32[321,3072]{1,0:T(8,128)}, ...), condition=%wide.region_15.16_spmd, body=%wide.region_13.15_spmd.sunk | while | flops 403440000 | bytes 9571999 | solution.py:69
  252.5 2.6 convolution_multiply_fusion.2
  255.1 6.6 %scatter_fusion = f32[321,3072]{1,0:T(8,128)} fusion(f32[321,3072]{1,0:T(8,128)} %get-tuple-element.242, s32[128]{0:T(128)S(1)} %fusion.64, f32[128,3072]{1,0:T(8,128)S(1)} %convolution_multiply_fusion.2), kind=kCustom, calls=%fused_computation.1.clone.1 | custom fusion | flops 393216 | bytes 4719104 | tf_op jit(solution)/shard_map/while/body/eval_jaxpr/scatter-add | solution.py:65
  266.8 6.6 %scatter_fusion = f32[321,3072]{1,0:T(8,128)} fusion(f32[321,3072]{1,0:T(8,128)} %get-tuple-element.242, s32[128]{0:T(128)S(1)} %fusion.64, f32[128,3072]{1,0:T(8,128)S(1)} %convolution_multiply_fusion.2), kind=kCustom, calls=%fused_computation.1.clone.1 | custom fusion | flops 393216 | bytes 4719104 | tf_op jit(solution)/shard_map/while/body/eval_jaxpr/scatter-add | solution.py:65
  276.0 2.6 convolution_multiply_fusion.2
  278.6 6.6 %scatter_fusion = f32[321,3072]{1,0:T(8,128)} fusion(f32[321,3072]{1,0:T(8,128)} %get-tuple-element.242, s32[128]{0:T(128)S(1)} %fusion.64, f32[128,3072]{1,0:T(8,128)S(1)} %convolution_multiply_fusion.2), kind=kCustom, calls=%fused_computation.1.clone.1 | custom fusion | flops 393216 | bytes 4719104 | tf_op jit(solution)/shard_map/while/body/eval_jaxpr/scatter-add | solution.py:65
  287.7 2.6 convolution_multiply_fusion.2
  290.3 6.6 %scatter_fusion = f32[321,3072]{1,0:T(8,128)} fusion(f32[321,3072]{1,0:T(8,128)} %get-tuple-element.242, s32[128]{0:T(128)S(1)} %fusion.64, f32[128,3072]{1,0:T(8,128)S(1)} %convolution_multiply_fusion.2), kind=kCustom, calls=%fused_computation.1.clone.1 | custom fusion | flops 393216 | bytes 4719104 | tf_op jit(solution)/shard_map/while/body/eval_jaxpr/scatter-add | solution.py:65
  302.0 6.6 %scatter_fusion = f32[321,3072]{1,0:T(8,128)} fusion(f32[321,3072]{1,0:T(8,128)} %get-tuple-element.242, s32[128]{0:T(128)S(1)} %fusion.64, f32[128,3072]{1,0:T(8,128)S(1)} %convolution_multiply_fusion.2), kind=kCustom, calls=%fused_computation.1.clone.1 | custom fusion | flops 393216 | bytes 4719104 | tf_op jit(solution)/shard_map/while/body/eval_jaxpr/scatter-add | solution.py:65
  313.7 6.6 %scatter_fusion = f32[321,3072]{1,0:T(8,128)} fusion(f32[321,3072]{1,0:T(8,128)} %get-tuple-element.242, s32[128]{0:T(128)S(1)} %fusion.64, f32[128,3072]{1,0:T(8,128)S(1)} %convolution_multiply_fusion.2), kind=kCustom, calls=%fused_computation.1.clone.1 | custom fusion | flops 393216 | bytes 4719104 | tf_op jit(solution)/shard_map/while/body/eval_jaxpr/scatter-add | solution.py:65
  325.4 6.6 %scatter_fusion = f32[321,3072]{1,0:T(8,128)} fusion(f32[321,3072]{1,0:T(8,128)} %get-tuple-element.242, s32[128]{0:T(128)S(1)} %fusion.64, f32[128,3072]{1,0:T(8,128)S(1)} %convolution_multiply_fusion.2), kind=kCustom, calls=%fused_computation.1.clone.1 | custom fusion | flops 393216 | bytes 4719104 | tf_op jit(solution)/shard_map/while/body/eval_jaxpr/scatter-add | solution.py:65
  337.2 6.6 %scatter_fusion = f32[321,3072]{1,0:T(8,128)} fusion(f32[321,3072]{1,0:T(8,128)} %get-tuple-element.242, s32[128]{0:T(128)S(1)} %fusion.64, f32[128,3072]{1,0:T(8,128)S(1)} %convolution_multiply_fusion.2), kind=kCustom, calls=%fused_computation.1.clone.1 | custom fusion | flops 393216 | bytes 4719104 | tf_op jit(solution)/shard_map/while/body/eval_jaxpr/scatter-add | solution.py:65
  348.9 6.6 %scatter_fusion = f32[321,3072]{1,0:T(8,128)} fusion(f32[321,3072]{1,0:T(8,128)} %get-tuple-element.242, s32[128]{0:T(128)S(1)} %fusion.64, f32[128,3072]{1,0:T(8,128)S(1)} %convolution_multiply_fusion.2), kind=kCustom, calls=%fused_computation.1.clone.1 | custom fusion | flops 393216 | bytes 4719104 | tf_op jit(solution)/shard_map/while/body/eval_jaxpr/scatter-add | solution.py:65
  355.5 4.5 %slice.11 = f32[320,3072]{1,0:T(8,128)} slice(f32[321,3072]{1,0:T(8,128)} %get-tuple-element.82), slice={[0:320], [0:3072]} | slice | bytes 7864320 | tf_op jit(solution)/shard_map/slice | solution.py:72
  359.9 57.1 %fusion = f32[24,3072]{1,0:T(8,128)S(1)} fusion(f32[320,3072]{1,0:T(8,128)} %slice.11), kind=kCustom, calls=%all-reduce-scatter | all-reduce-scatter fusion | flops 1179649 | bytes 4227584
  418.4 2.9 collective-permute-start.1
  421.4 4.4 %collective-permute-start.2 = (bf16[12,3072]{1,0:T(8,128)(2,1)S(1)}, bf16[12,3072]{1,0:T(8,128)(2,1)S(1)}, u32[]{:S(2)}, u32[]{:S(2)}) collective-permute-start(bf16[12,3072]{1,0:T(8,128)(2,1)S(1)} %slice.15), channel_id=1, source_target_pairs={{0,6},{2,8},{4,10},{6,12},{8,14},{10,16},{12,18},{14,20},{16,22},{... | collective-permute-start | bytes 221192
  (90 shorter events, 49.3 us)
Async XLA Ops:
  6.5 48.1 %all-gather.6.cloned.1.call-start = ((), (), s32[]{:S(2)}) async-start(), calls=%async_computation.3 | async-start | bytes 2506752 | tf_op jit(solution)/shard_map/all_gather | solution.py:10
  156.6 32.1 %all-to-all-start = ((f32[1,1152,512]{2,0,1:T(1,128)}), f32[1,1152,512]{2,0,1:T(1,128)S(1)}, u32[]{:S(2)}, u32[]{:S(2)}) async-start(f32[1,1152,512]{2,0,1:T(1,128)} %broadcast_in_dim_reshape.7), calls=%async_computation | async-start | bytes 4718592 | tf_op jit(solution)/shard_map/all_to_all | solution.py:50
  188.7 32.5 %all-to-all-start.1 = ((f32[1,1152,512]{2,0,1:T(1,128)}), f32[1,1152,512]{2,0,1:T(1,128)}, u32[]{:S(2)}, u32[]{:S(2)}) async-start(f32[1,1152,512]{2,0,1:T(1,128)} %broadcast_in_dim_reshape.8), calls=%async_computation.1 | async-start | bytes 4718592 | tf_op jit(solution)/shard_map/all_to_all | solution.py:51
  193.7 54.0 %all-gather.4.cloned.1.call-start = ((), (), s32[]{:S(2)}) async-start(), calls=%async_computation.2 | async-start | bytes 1769472 | tf_op jit(solution)/shard_map/all_gather | solution.py:56
  224.4 2.5 copy-start
  359.9 65.8 %copy-start.1 = (u32[32]{0:T(128)S(1)}, u32[32]{0:T(128)}, u32[]{:S(2)}) copy-start(u32[32]{0:T(128)} %constant.105) | copy-start | bytes 388
  417.1 10.9 %collective-permute-start = (bf16[24,3072]{1,0:T(8,128)(2,1)S(1)}, bf16[24,3072]{1,0:T(8,128)(2,1)S(1)}, u32[]{:S(2)}, u32[]{:S(2)}) collective-permute-start(bf16[24,3072]{1,0:T(8,128)(2,1)S(1)} %convert.18), channel_id=1, source_target_pairs={{0,2},{2,4},{4,6},{6,8},{8,10},{10,12},{12,14},{14,16},{16,18},{18... | collective-permute-start | bytes 442376
  418.4 9.6 %collective-permute-start.1 = (bf16[24,3072]{1,0:T(8,128)(2,1)S(1)}, bf16[24,3072]{1,0:T(8,128)(2,1)S(1)}, u32[]{:S(2)}, u32[]{:S(2)}) collective-permute-start(bf16[24,3072]{1,0:T(8,128)(2,1)S(1)} %convert.18), channel_id=1, source_target_pairs={{0,4},{2,6},{4,8},{6,10},{8,12},{10,14},{12,16},{14,18},{16,20},{1... | collective-permute-start | bytes 442376
  421.4 6.6 %collective-permute-start.2 = (bf16[12,3072]{1,0:T(8,128)(2,1)S(1)}, bf16[12,3072]{1,0:T(8,128)(2,1)S(1)}, u32[]{:S(2)}, u32[]{:S(2)}) collective-permute-start(bf16[12,3072]{1,0:T(8,128)(2,1)S(1)} %slice.15), channel_id=1, source_target_pairs={{0,6},{2,8},{4,10},{6,12},{8,14},{10,16},{12,18},{14,20},{16,22},{... | collective-permute-start | bytes 221192
Sparse Core Ops, SparseCore 0:
  9.6 45.0 all-gather.5
  227.0 20.5 all-gather.3
where the time goes:
time: 440 us; the launch traced here: 436 us
  waiting for transfers between devices  105 us (24%)
  matrix products  84.9 us (19%)
  other arithmetic  67.2 us (15%)
  blocking collectives  57.1 us (13%)
  local copies, waits for them, and re-layouts  56.5 us (13%)
  loops' own time  34.1 us (8%)
  starting transfers between devices  17.4 us (4%)
  between operations  14.3 us (3%)
    scatter-add x9, other arithmetic, second_pass(): mixed_acc.at[block_source].add(out_block * block_weight[:, None])  59.3 us
    unnamed x1, blocking collectives  57.1 us
    all_gather x1, waiting for transfers between devices, local(): all_tokens = lax.all_gather(tokens, 'dp', axis=0, tiled=True)  40 us
    dot_general x9, matrix products, first_pass(): jnp.dot(block_tokens, up_weight, preferred_element_type=jnp.float32)  31 us
    dot_general x9, matrix products, first_pass(): jnp.dot(block_tokens, gate_weight, preferred_element_type=jnp.float32)  30.9 us
    all_to_all x1, waiting for transfers between devices, local(): lax.all_to_all(up_part[None], 'tensor', split_axis=1, concat_axis=0, tile...  23.8 us
    all_to_all x1, waiting for transfers between devices, local(): lax.all_to_all(gate_part[None], 'tensor', split_axis=1, concat_axis=0, ti...  23.4 us
    dot_general x9, matrix products, second_pass(): jnp.dot(block_hidden, down_weight, preferred_element_type=jnp.float32)  23 us
  transfers between devices with their start and end apart: 7, of which 5 were waited for; matrix products, arithmetic and copies ran while one was open for 5% of the time, Pallas kernels for 0%

commit v1 on v0

v1 whole, which is shorter than its diff:
```python
import functools

import jax
import jax.numpy as jnp
from jax import lax
from jax.experimental import pallas as pl
from jax.experimental.pallas import tpu as pltpu
from jax.sharding import PartitionSpec as P

BF = jnp.bfloat16
F32 = jnp.float32


def tile_of(width, most):
    tile = min(width, most)
    while width % tile:
        tile //= 2
    return tile


def up_kernel(n, where_ref, ids_ref, own_ref, other_ref, wg_ref, wu_ref, keep_ref, send_ref, acc_ref):
    e = pl.program_id(1)
    half, me = where_ref[0], where_ref[1]
    top = ids_ref.shape[1]
    rows = keep_ref.shape[2]
    for which, w_ref in enumerate((wg_ref, wu_ref)):
        part = jnp.dot(own_ref[...], w_ref[0, half], preferred_element_type=F32)
        part += jnp.dot(other_ref[...], w_ref[0, 1 - half], preferred_element_type=F32)
        for k in range(top):
            chosen = ids_ref[:, k : k + 1] == e
            acc_ref[which, k] = jnp.where(chosen, part, acc_ref[which, k])

    @pl.when(e == pl.num_programs(1) - 1)
    def _():
        for s in range(n):
            begin = pl.multiple_of(lax.rem(me + s, n) * rows, rows)
            block = acc_ref[:, :, pl.ds(begin, rows), :]
            if s == 0:
                keep_ref[...] = block
            else:
                send_ref[s - 1] = block.astype(BF)


def up_gemm(n, where, ids, own, other, w_gate, w_up):
    token_count, top = ids.shape
    experts, width, hidden = w_gate.shape
    half = own.shape[1]
    tile = tile_of(hidden, 256)
    rows = token_count // n
    weight = pl.BlockSpec((1, 2, half, tile), lambda j, e, w: (e, 0, 0, j))
    tokens = pl.BlockSpec((token_count, half), lambda j, e, w: (0, 0))
    return pl.pallas_call(
        functools.partial(up_kernel, n),
        grid_spec=pltpu.PrefetchScalarGridSpec(
            num_scalar_prefetch=1,
            grid=(hidden // tile, experts),
            in_specs=[
                pl.BlockSpec((token_count, top), lambda j, e, w: (0, 0)),
                tokens,
                tokens,
                weight,
                weight,
            ],
            out_specs=[
                pl.BlockSpec((2, top, rows, tile), lambda j, e, w: (0, 0, 0, j)),
                pl.BlockSpec((n - 1, 2, top, rows, tile), lambda j, e, w: (0, 0, 0, 0, j)),
            ],
            scratch_shapes=[pltpu.VMEM((2, top, token_count, tile), F32)],
        ),
        out_shape=[
            jax.ShapeDtypeStruct((2, top, rows, hidden), F32),
            jax.ShapeDtypeStruct((n - 1, 2, top, rows, hidden), BF),
        ],
        cost_estimate=pl.CostEstimate(
            flops=4 * token_count * width * hidden * experts,
            bytes_accessed=4 * experts * width * hidden,
            transcendentals=0,
        ),
        name="up_gemm",
    )(where, ids, own, other, w_gate.reshape(experts, 2, half, hidden), w_up.reshape(experts, 2, half, hidden))


def down_kernel(n, where_ref, ids_ref, probs_ref, *refs):
    hidden_refs, (wd_ref, out_ref, rows_ref) = refs[:n], refs[n:]
    me = where_ref[1]
    experts = wd_ref.shape[0]
    top, rows = hidden_refs[0].shape[:2]

    @pl.when(pl.program_id(0) == 0)
    def _():
        for s in range(n):
            begin = pl.multiple_of(lax.rem(me + n - s, n) * rows, rows)
            for e in range(experts):
                total = jnp.zeros(hidden_refs[s].shape[1:], F32)
                for k in range(top):
                    chosen = ids_ref[pl.ds(begin, rows), k : k + 1] == e
                    total = jnp.where(chosen, hidden_refs[s][k].astype(F32), total)
                rows_ref[e, pl.ds(begin, rows), :] = total.astype(BF)

    mixed = None
    for e in range(experts):
        share = jnp.zeros((ids_ref.shape[0], 1), F32)
        for k in range(top):
            share = jnp.where(ids_ref[:, k : k + 1] == e, probs_ref[:, k : k + 1], share)
        term = share * jnp.dot(rows_ref[e], wd_ref[e], preferred_element_type=F32)
        mixed = term if mixed is None else mixed + term
    out_ref[...] = mixed.astype(out_ref.dtype)


def down_gemm(n, where, ids, probs, hiddens, w_down, own, dtype):
    token_count, top = ids.shape
    experts, hidden, width = w_down.shape
    half = width // 2
    tile = tile_of(half, 512)
    tiles = half // tile
    rows = token_count // n
    small = pl.BlockSpec((token_count, top), lambda j, w: (0, 0))

    def column(j, w):
        side = w[0] if own else 1 - w[0]
        return (0, 0, side * tiles + j)

    return pl.pallas_call(
        functools.partial(down_kernel, n),
        grid_spec=pltpu.PrefetchScalarGridSpec(
            num_scalar_prefetch=1,
            grid=(tiles,),
            in_specs=[small, small]
            + [pl.BlockSpec((top, rows, hidden), lambda j, w: (0, 0, 0))] * n
            + [pl.BlockSpec((experts, hidden, tile), column)],
            out_specs=pl.BlockSpec((token_count, tile), lambda j, w: (0, j)),
            scratch_shapes=[pltpu.VMEM((experts, token_count, hidden), BF)],
        ),
        out_shape=jax.ShapeDtypeStruct((token_count, half), dtype),
        cost_estimate=pl.CostEstimate(
            flops=2 * token_count * half * hidden * experts,
            bytes_accessed=2 * experts * half * hidden,
            transcendentals=0,
        ),
        name="down_own" if own else "down_other",
    )(where, ids, probs, *hiddens, w_down)


def local(tokens, route_ids, route_probs, w_gate, w_up, w_down):
    members = lax.axis_size("dp")
    n = lax.axis_size("tensor")
    chips = members // 2
    swap = [(i, i ^ 1) for i in range(members)]
    planes = [[2 * i + c for i in range(chips)] for c in range(2)]
    side = lax.axis_index("dp") % 2
    me = lax.axis_index("tensor")
    where = jnp.stack([side, me]).astype(jnp.int32)
    local_rows, width = tokens.shape
    half = width // 2
    first = side == 0
    probs = route_probs.astype(F32)

    def on_chip(x):
        return lax.ppermute(x, "dp", swap)

    def pair(mine, theirs, axis):
        return jnp.concatenate(
            [jnp.where(first, mine, theirs), jnp.where(first, theirs, mine)], axis=axis
        )

    left, right = tokens[:, :half], tokens[:, half:]
    theirs = on_chip(jnp.where(first, right, left))
    block = pair(jnp.where(first, left, right), theirs, 0)
    own = lax.all_to_all(
        jnp.broadcast_to(block[None], (chips,) + block.shape), "dp", 0, 0, tiled=True, axis_index_groups=planes
    ).reshape(chips * 2 * local_rows, half)
    other = on_chip(own)

    keep, send = up_gemm(n, where, route_ids, own, other, w_gate, w_up)
    sums = keep
    for s in range(1, n):
        shift = [(i, (i + s) % n) for i in range(n)]
        sums = sums + lax.ppermute(send[s - 1], "tensor", shift).astype(F32)
    gate_sum, up_sum = sums[0], sums[1]
    hidden = (gate_sum * jax.nn.sigmoid(gate_sum) * up_sum).astype(BF)
    hiddens = [hidden]
    for s in range(1, n):
        shift = [(i, (i + s) % n) for i in range(n)]
        hiddens.append(lax.ppermute(hidden, "tensor", shift))

    away = on_chip(down_gemm(n, where, route_ids, probs, hiddens, w_down, False, BF))
    stay = down_gemm(n, where, route_ids, probs, hiddens, w_down, True, F32)
    parts = (stay + away.astype(F32)).astype(BF).reshape(chips, 2 * local_rows, half)
    terms = lax.all_to_all(parts, "dp", 0, 0, tiled=True, axis_index_groups=planes)
    mixed = jnp.sum(terms.astype(F32), axis=0).astype(BF)
    top, bottom = mixed[:local_rows], mixed[local_rows:]
    others = on_chip(jnp.where(first, bottom, top))
    return pair(jnp.where(first, top, bottom), others, 1)


def solution(mesh):
    placed = (
        P("dp", "tensor"),
        P(),
        P(),
        P(None, "tensor", "dp"),
        P(None, "tensor", "dp"),
        P(None, "dp", "tensor"),
    )
    return jax.shard_map(
        local, mesh=mesh, in_specs=placed, out_specs=P("dp", "tensor"), check_vma=False
    )
```

time: 440 us -> 132 us (0.30)
  matrix products: 84.9 us -> 0 us
  waiting for transfers between devices: 105 us -> 25.2 us
  other arithmetic: 67.2 us -> 7.61 us
  local copies, waits for them, and re-layouts: 56.5 us -> 2.9 us
  loops' own time: 34.1 us -> 0 us
  Pallas kernels: 0 us -> 31.6 us
  between operations: 14.3 us -> 0.08 us
  starting transfers between devices: 17.4 us -> 3.74 us
    dot_general x27 -> x0, matrix products: 84.9 us -> none  [the longest x9 31 us: first_pass(): jnp.dot(block_tokens, up_weight, preferred_element_type=jnp.float32)]
    all_to_all x0 -> x2, blocking collectives: none -> 60 us  [the longest x1 31.7 us: local(): lax.all_to_all(jnp.broadcast_to(block[None], (chips,) + block.shape), 'dp...]
    scatter-add x9 -> x0, other arithmetic: 59.3 us -> none  [second_pass(): mixed_acc.at[block_source].add(out_block * block_weight[:, None])]
    unnamed x1 -> x0, blocking collectives: 57.1 us -> none
    all_gather x2 -> x0, waiting for transfers between devices: 56.1 us -> none  [the longest x1 40 us: local(): all_tokens = lax.all_gather(tokens, 'dp', axis=0, tiled=True)]
    all_to_all x2 -> x0, waiting for transfers between devices: 47.2 us -> none  [the longest x1 23.8 us: local(): lax.all_to_all(up_part[None], 'tensor', split_axis=1, concat_axis=0, tile...]
    another operation x2 -> x0, loops' own time: 34.1 us -> none  [the longest x1 17.2 us: local(): lax.scan(second_pass, start_acc, (hidden_blocks, source_blocks, weight_bl...]
    pallas_call x0 -> x3, Pallas kernels: none -> 31.6 us  [the longest x1 16.8 us: up_gemm(): pl.pallas_call(functools.partial(up_kernel, n), grid_spec=pltpu.PrefetchS...]
  transfers between devices with their start and end apart: 7 -> 6, of which waited for: 5 -> 5; matrix products, arithmetic and copies ran while one was open for 5% -> 2% of each run, Pallas kernels for 0% -> 6%
where the time goes in v1:
time: 132 us; the launch traced here: 131 us
  blocking collectives  60 us (45%)
  Pallas kernels  31.6 us (24%)
  waiting for transfers between devices  25.2 us (19%)
  other arithmetic  7.61 us (6%)
  starting transfers between devices  3.74 us (3%)
  local copies, waits for them, and re-layouts  2.9 us (2%)
    all_to_all x1, blocking collectives, local(): lax.all_to_all(jnp.broadcast_to(block[None], (chips,) + block.shape), 'dp...  31.7 us
    all_to_all x1, blocking collectives, local(): lax.all_to_all(parts, 'dp', 0, 0, tiled=True, axis_index_groups=planes)  28.4 us
    pallas_call x1, Pallas kernels, up_gemm(): pl.pallas_call(functools.partial(up_kernel, n), grid_spec=pltpu.PrefetchS...  16.8 us
    ppermute x1, waiting for transfers between devices, local(): sums = sums + lax.ppermute(send[s - 1], 'tensor', shift).astype(F32)  15.5 us
    pallas_call x2, Pallas kernels, down_gemm(): pl.pallas_call(functools.partial(down_kernel, n), grid_spec=pltpu.Prefetc...  14.8 us
    ppermute x1, waiting for transfers between devices, local(): hiddens.append(lax.ppermute(hidden, 'tensor', shift))  6.53 us
    ppermute x4, waiting for transfers between devices, on_chip(): return lax.ppermute(x, 'dp', swap)  3.17 us
    unnamed x14, local copies, waits for them, and re-layouts  2.84 us
  transfers between devices with their start and end apart: 6, of which 5 were waited for; matrix products, arithmetic and copies ran while one was open for 2% of the time, Pallas kernels for 6%

profile of v1, /device:TPU:0, one launch (start us, length us, event | category | flops | bytes accessed | tf_op | source)
XLA Modules:
  0.0 131.1 jit_solution(12210246896245102255)
XLA Ops:
  0.0 0.0 copy-start.3
  0.0 0.9 broadcast_select_fusion.6
  0.9 0.6 collective-permute-start
  1.5 0.9 collective-permute-done
  2.4 0.9 broadcast_select_fusion.5
  3.4 0.1 broadcast_in_dim.2
  3.5 31.7 %all_to_all.10 = bf16[8,40,1536]{2,1,0:T(8,128)(2,1)S(1)} all-to-all(bf16[8,40,1536]{2,1,0:T(8,128)(2,1)S(1)} %broadcast_in_dim.2), channel_id=1, replica_groups={{0,4,8,12,16,20,24,28},{2,6,10,14,18,22,26,30},{1,5,9,13,17,21,25,29},{..., dimensions={0} | all-to-all | bytes 1966080 | tf_op jit(solution)/shard_map/all_to_all | solution.py:169
  35.2 0.0 copy-start.2
  35.2 0.0 collective-permute-start.1
  35.2 0.0 copy-done.3
  35.2 1.0 copy.9.ids_ref
  36.1 0.6 pad_add_fusion.where_ref
  36.7 1.0 collective-permute-done.1.other_ref
  37.7 0.0 copy-start.5
  37.7 0.0 copy-done.2
  37.7 1.0 copy-done.5
  38.7 16.8 %up_gemm.1 = (f32[2,2,160,512]{3,2,1,0:T(8,128)}, bf16[1,2,2,160,512]{4,3,2,1,0:T(8,128)(2,1)}) custom-call(s32[2]{0:T(128)} %pad_add_fusion.where_ref, s32[320,2]{1,0:T(8,128)} %copy.9.ids_ref, bf16[320,1536]{1,0:T(8,128)(2,1)} %bitcast.19, bf16[320,1536]{1,0:T(8,128)(2,1)} %copy-done.5, bf16[4,2,1536,512]{3,2,1,0:T(8,128)(2,1)} %bitcast.20, ...), custom_call_target="tpu_custom_call" | custom-call | flops 8053063680 | bytes 25165824 | tf_op jit(solution)/shard_map/up_gemm/pallas_call | solution.py:52
  55.5 1.5 %collective-permute-start.2 = (bf16[2,2,160,512]{3,2,1,0:T(8,128)(2,1)}, bf16[2,2,160,512]{3,2,1,0:T(8,128)(2,1)S(1)}, u32[]{:S(2)}, u32[]{:S(2)}) collective-permute-start(bf16[2,2,160,512]{3,2,1,0:T(8,128)(2,1)} %bitcast.22), channel_id=1, source_target_pairs={{0,1},{1,0},{2,3},{3,2},{4,5},{5,4},{6,7},{7,6},{8,9},{9,8},{10,11... | collective-permute-start | bytes 1966088 | tf_op jit(solution)/shard_map/ppermute | solution.py:178
  57.0 15.5 %collective-permute-done.2 = bf16[2,2,160,512]{3,2,1,0:T(8,128)(2,1)S(1)} collective-permute-done((bf16[2,2,160,512]{3,2,1,0:T(8,128)(2,1)}, bf16[2,2,160,512]{3,2,1,0:T(8,128)(2,1)S(1)}, u32[]{:S(2)}, u32[]{:S(2)}) %collective-permute-start.2) | collective-permute-done | bytes 655392 | tf_op jit(solution)/shard_map/ppermute | solution.py:178
  72.5 0.0 copy-start.4
  72.5 1.6 %convert_add_fusion = f32[2,2,160,512]{3,2,1,0:T(8,128)S(1)} fusion(f32[2,2,160,512]{3,2,1,0:T(8,128)} %get-tuple-element.7, bf16[2,2,160,512]{3,2,1,0:T(8,128)(2,1)S(1)} %collective-permute-done.2), kind=kLoop, calls=%fused_computation.1 | loop fusion | flops 655360 | bytes 3276800 | tf_op jit(solution)/shard_map/add | solution.py:178
  74.0 0.2 fusion.1.refs_0_
  74.2 0.0 copy-start
  74.2 1.6 %collective-permute-start.3 = (bf16[2,160,512]{2,1,0:T(8,128)(2,1)S(1)}, bf16[2,160,512]{2,1,0:T(8,128)(2,1)S(1)}, u32[]{:S(2)}, u32[]{:S(2)}) collective-permute-start(bf16[2,160,512]{2,1,0:T(8,128)(2,1)S(1)} %fusion.1.refs_0_), channel_id=1, source_target_pairs={{0,1},{1,0},{2,3},{3,2},{4,5},{5,4},{6,7},{7,6},{8,9},{9,8},{10,11... | collective-permute-start | bytes 983048 | tf_op jit(solution)/shard_map/ppermute | solution.py:184
  75.8 0.0 copy-done.4
  75.8 0.2 copy.7
  76.0 0.7 convert_element_type.17.probs_ref
  76.7 6.5 %collective-permute-done.3.refs_1_ = bf16[2,160,512]{2,1,0:T(8,128)(2,1)S(1)} collective-permute-done((bf16[2,160,512]{2,1,0:T(8,128)(2,1)S(1)}, bf16[2,160,512]{2,1,0:T(8,128)(2,1)S(1)}, u32[]{:S(2)}, u32[]{:S(2)}) %collective-permute-start.3) | collective-permute-done | bytes 327712 | tf_op jit(solution)/shard_map/ppermute | solution.py:184
  83.2 0.0 copy-done
  83.2 0.0 copy-start.1
  83.2 0.7 copy-done.1
  83.9 7.3 %down_other.1 = bf16[320,1536]{1,0:T(8,128)(2,1)} custom-call(s32[2]{0:T(128)} %pad_add_fusion.where_ref, s32[320,2]{1,0:T(8,128)} %copy.9.ids_ref, f32[320,2]{1,0:T(8,128)} %convert_element_type.17.probs_ref, bf16[2,160,512]{2,1,0:T(8,128)(2,1)} %copy-done, bf16[2,160,512]{2,1,0:T(8,128)(2,1)} %copy-done.1, bf16[4,512,3072]{2,1,0:T(8,128)(2,1)} %refs_2_.3), custom_call_target="tpu_custom_call" | custom-call | flops 2013265920 | bytes 6291456 | tf_op jit(solution)/shard_map/down_other/pallas_call | solution.py:123
  91.2 0.0 collective-permute-start.4
  91.2 7.5 %down_own.1 = f32[320,1536]{1,0:T(8,128)} custom-call(s32[2]{0:T(128)} %pad_add_fusion.where_ref, s32[320,2]{1,0:T(8,128)} %copy.9.ids_ref, f32[320,2]{1,0:T(8,128)} %convert_element_type.17.probs_ref, bf16[2,160,512]{2,1,0:T(8,128)(2,1)} %copy-done, bf16[2,160,512]{2,1,0:T(8,128)(2,1)} %copy-done.1, bf16[4,512,3072]{2,1,0:T(8,128)(2,1)} %refs_2_.3), custom_call_target="tpu_custom_call" | custom-call | flops 2013265920 | bytes 6291456 | tf_op jit(solution)/shard_map/down_own/pallas_call | solution.py:123
  98.8 0.0 collective-permute-done.4
  98.8 1.8 %add_convert_fusion = bf16[320,1536]{1,0:T(8,128)(2,1)S(1)} fusion(f32[320,1536]{1,0:T(8,128)} %down_own.1, bf16[320,1536]{1,0:T(8,128)(2,1)S(1)} %collective-permute-done.4), kind=kLoop, calls=%fused_computation | loop fusion | flops 1474560 | bytes 3932160 | tf_op jit(solution)/shard_map/convert_element_type | solution.py:188
  100.6 28.4 %all_to_all.11 = bf16[8,40,1536]{2,1,0:T(8,128)(2,1)S(1)} all-to-all(bf16[8,40,1536]{2,1,0:T(8,128)(2,1)S(1)} %bitcast.17), channel_id=1, replica_groups={{0,4,8,12,16,20,24,28},{2,6,10,14,18,22,26,30},{1,5,9,13,17,21,25,29},{..., dimensions={0} | all-to-all | bytes 1966080 | tf_op jit(solution)/shard_map/all_to_all | solution.py:189
  128.9 0.1 reduce_sum.12
  129.1 0.1 collective-permute-start.5
  129.2 1.3 collective-permute-done.5
  130.5 0.7 pad_maximum_fusion
  (3 shorter events, 0.1 us)
Async XLA Ops:
  0.0 35.2 %copy-start.3 = (s32[320,2]{0,1:T(2,128)S(1)}, s32[320,2]{0,1:T(2,128)}, u32[]{:S(2)}) copy-start(s32[320,2]{0,1:T(2,128)} %param.7) | copy-start | bytes 7684
  0.9 1.5 %collective-permute-start = (bf16[20,1536]{1,0:T(8,128)(2,1)S(1)}, bf16[20,1536]{1,0:T(8,128)(2,1)S(1)}, u32[]{:S(2)}, u32[]{:S(2)}) collective-permute-start(bf16[20,1536]{1,0:T(8,128)(2,1)S(1)} %broadcast_select_fusion.6), channel_id=1, source_target_pairs={{0,2},{2,0},{4,6},{6,4},{8,10},{10,8},{12,14},{14,12},{16,18},{18,... | collective-permute-start | bytes 184328 | tf_op jit(solution)/shard_map/ppermute | solution.py:159
  35.2 2.6 %copy-start.2 = (bf16[8,40,1536]{2,1,0:T(8,128)(2,1)}, bf16[8,40,1536]{2,1,0:T(8,128)(2,1)S(1)}, u32[]{:S(2)}) copy-start(bf16[8,40,1536]{2,1,0:T(8,128)(2,1)S(1)} %all_to_all.10) | copy-start | bytes 2949124
  35.2 2.6 %collective-permute-start.1 = (bf16[320,1536]{1,0:T(8,128)(2,1)S(1)}, bf16[320,1536]{1,0:T(8,128)(2,1)S(1)}, u32[]{:S(2)}, u32[]{:S(2)}) collective-permute-start(bf16[320,1536]{1,0:T(8,128)(2,1)S(1)} %bitcast.18), channel_id=1, source_target_pairs={{0,2},{2,0},{4,6},{6,4},{8,10},{10,8},{12,14},{14,12},{16,18},{18,... | collective-permute-start | bytes 2949128 | tf_op jit(solution)/shard_map/ppermute | solution.py:159
  37.7 1.0 copy-start.5
  55.5 17.0 %collective-permute-start.2 = (bf16[2,2,160,512]{3,2,1,0:T(8,128)(2,1)}, bf16[2,2,160,512]{3,2,1,0:T(8,128)(2,1)S(1)}, u32[]{:S(2)}, u32[]{:S(2)}) collective-permute-start(bf16[2,2,160,512]{3,2,1,0:T(8,128)(2,1)} %bitcast.22), channel_id=1, source_target_pairs={{0,1},{1,0},{2,3},{3,2},{4,5},{5,4},{6,7},{7,6},{8,9},{9,8},{10,11... | collective-permute-start | bytes 1966088 | tf_op jit(solution)/shard_map/ppermute | solution.py:178
  72.5 3.4 %copy-start.4 = (bf16[320,2]{0,1:T(2,128)(2,1)S(1)}, bf16[320,2]{0,1:T(2,128)(2,1)}, u32[]{:S(2)}) copy-start(bf16[320,2]{0,1:T(2,128)(2,1)} %param.8) | copy-start | bytes 3844
  74.2 9.0 %copy-start = (bf16[2,160,512]{2,1,0:T(8,128)(2,1)}, bf16[2,160,512]{2,1,0:T(8,128)(2,1)S(1)}, u32[]{:S(2)}) copy-start(bf16[2,160,512]{2,1,0:T(8,128)(2,1)S(1)} %fusion.1.refs_0_) | copy-start | bytes 983044
  74.2 9.0 %collective-permute-start.3 = (bf16[2,160,512]{2,1,0:T(8,128)(2,1)S(1)}, bf16[2,160,512]{2,1,0:T(8,128)(2,1)S(1)}, u32[]{:S(2)}, u32[]{:S(2)}) collective-permute-start(bf16[2,160,512]{2,1,0:T(8,128)(2,1)S(1)} %fusion.1.refs_0_), channel_id=1, source_target_pairs={{0,1},{1,0},{2,3},{3,2},{4,5},{5,4},{6,7},{7,6},{8,9},{9,8},{10,11... | collective-permute-start | bytes 983048 | tf_op jit(solution)/shard_map/ppermute | solution.py:184
  83.2 0.7 copy-start.1
  91.2 7.5 %collective-permute-start.4 = (bf16[320,1536]{1,0:T(8,128)(2,1)}, bf16[320,1536]{1,0:T(8,128)(2,1)S(1)}, u32[]{:S(2)}, u32[]{:S(2)}) collective-permute-start(bf16[320,1536]{1,0:T(8,128)(2,1)} %down_other.1), channel_id=1, source_target_pairs={{0,2},{2,0},{4,6},{6,4},{8,10},{10,8},{12,14},{14,12},{16,18},{18,... | collective-permute-start | bytes 2949128 | tf_op jit(solution)/shard_map/ppermute | solution.py:159
  129.1 1.3 %collective-permute-start.5 = (bf16[20,1536]{1,0:T(8,128)(2,1)S(1)}, bf16[20,1536]{1,0:T(8,128)(2,1)S(1)}, u32[]{:S(2)}, u32[]{:S(2)}) collective-permute-start(bf16[20,1536]{1,0:T(8,128)(2,1)S(1)} %broadcast_select_fusion.2), channel_id=1, source_target_pairs={{0,2},{2,0},{4,6},{6,4},{8,10},{10,8},{12,14},{14,12},{16,18},{18,... | collective-permute-start | bytes 184328 | tf_op jit(solution)/shard_map/ppermute | solution.py:159
